TPU v7x, 128 devices: a whole 4x4x4 slice. The times are simulated.
128 devices in a mesh: seq: 16 (over x_lo, y, core), tp: 8 (over z, x_hi).
Axes of the slice: x: 4 (x_hi: 2, x_lo: 2; x = x_hi * 2 + x_lo), y: 4, z: 4, core: 2. Of those that a mesh axis runs over, the one named last changes fastest.
Arguments:
- selected_hidden: bfloat16 [32, 104, 2048], P('seq', None, 'tp'), may hold values from -6 to 6
- cached_keys: bfloat16 [32, 1024, 1024], P('seq', None, 'tp'), may hold values from -48 to 48
- cached_values: bfloat16 [32, 1024, 1024], P('seq', None, 'tp'), may hold values from -6 to 6
- slot_spans: int32 [32], replicated, may hold values from 0 to 31, each once
- span_order: int32 [4, 8], replicated, may hold values from 0 to 7, each once within a row
- cache_start: int32 [4, 8], replicated, may hold values from 0 to 16383
- selected_index: int32 [32, 104], replicated, may hold values from 0 to 1023, as said below
- input_gain: bfloat16 [2048], replicated, may hold values from 0.5 to 2
- query_weight: bfloat16 [2048, 2048], P(None, 'tp'), may hold values from -0.125 to 0.125
- key_weight: bfloat16 [2048, 1024], P(None, 'tp'), may hold values from -0.125 to 0.125
- value_weight: bfloat16 [2048, 1024], P(None, 'tp'), may hold values from -0.125 to 0.125
- query_gain: bfloat16 [128], replicated, may hold values from 1 to 2
- key_gain: bfloat16 [128], replicated, may hold values from 1 to 2
- output_weight: bfloat16 [2048, 2048], P('tp'), may hold values from -0.125 to 0.125
- post_gain: bfloat16 [2048], replicated, may hold values from 0.5 to 2
- gate_weight: bfloat16 [2048, 6144], P(None, 'tp'), may hold values from -0.125 to 0.125
- up_weight: bfloat16 [2048, 6144], P(None, 'tp'), may hold values from -0.125 to 0.125
- down_weight: bfloat16 [6144, 2048], P('tp'), may hold values from -0.078125 to 0.078125
Outputs:
- new_hidden: bfloat16 [32, 104, 2048], P('seq', None, 'tp')
Inputs may be any that keep to these rules, and one draw needn't show every extreme that they name: `selected_index`: each row holds 104 distinct positions in increasing order. `slot_spans`: each span of each request is held by exactly one slot. `span_order`: each row places the 8 spans of a request in some order.
All inputs are finite; a program needn't handle non-finite values.
Results may differ from a plain program's by a relative error of at most 0.027.
Values may be sent and summed in bfloat16 or wider, within the bound.
No kernel may reach another device: no remote copies, remote signals or barrier semaphores. Data moves between devices by JAX's collectives and lax.ppermute only.
A program may use at most 128 MiB of HBM per device.

v0:
```python
import jax
import jax.numpy as jnp
from jax import lax
from jax.sharding import PartitionSpec as P

theta_base = 1000000.0
norm_eps = 1e-06


def rms_scale(values):
    return values * lax.rsqrt(jnp.mean(values * values, axis=-1, keepdims=True) + norm_eps)


def rotary(values, positions):
    half_len = values.shape[-1] // 2
    frequency = jnp.exp(
        -jnp.log(theta_base) * jnp.arange(half_len, dtype=jnp.float32) * 2.0 / values.shape[-1]
    )
    angles = positions.astype(jnp.float32)[..., None] * frequency
    cosine = jnp.cos(angles)[..., None, :]
    sine_part = jnp.sin(angles)[..., None, :]
    lower_half = values[..., :half_len]
    upper_half = values[..., half_len:]
    return jnp.concatenate(
        [
            lower_half * cosine - upper_half * sine_part,
            upper_half * cosine + lower_half * sine_part,
        ],
        axis=-1,
    )


def slot_table(slot_ids, slot_spans, span_order, cache_start, span_len):
    slot_count = slot_spans.shape[0]
    span_count = span_order.shape[1]
    slot_match = (slot_ids[:, None] == jnp.arange(slot_count, dtype=jnp.int32)[None, :]).astype(
        jnp.int32
    )
    span_ids = jnp.sum(slot_match * slot_spans[None, :], axis=1)
    span_match = (
        span_ids[:, None] == jnp.arange(span_order.size, dtype=jnp.int32)[None, :]
    ).astype(jnp.int32)
    new_place = jnp.sum(span_match * span_order.reshape(-1)[None, :], axis=1)
    old_start = jnp.sum(span_match * cache_start.reshape(-1)[None, :], axis=1)
    return (span_ids // span_count, new_place * span_len, old_start)


def on_device(
    selected_hidden,
    cached_keys,
    cached_values,
    slot_spans,
    span_order,
    cache_start,
    selected_index,
    input_gain,
    query_weight,
    key_weight,
    value_weight,
    query_gain,
    key_gain,
    output_weight,
    post_gain,
    gate_weight,
    up_weight,
    down_weight,
):
    slot_local, select_count, width_local = selected_hidden.shape
    span_len = cached_keys.shape[1]
    head_dim = query_gain.shape[0]
    kv_local = cached_keys.shape[2] // head_dim
    query_local = query_weight.shape[1] // head_dim
    group_size = query_local // kv_local
    row_count = slot_local * select_count
    score_scale = head_dim ** (-0.5)
    first_slot = lax.axis_index("seq") * slot_local
    local_slots = first_slot + jnp.arange(slot_local, dtype=jnp.int32)
    local_request, local_base, local_start = slot_table(
        local_slots, slot_spans, span_order, cache_start, span_len
    )
    local_index = lax.dynamic_slice_in_dim(selected_index, first_slot, slot_local, 0)
    query_pos = (local_base[:, None] + local_index).reshape(-1)
    query_request = jnp.broadcast_to(local_request[:, None], (slot_local, select_count)).reshape(-1)
    hidden_local = selected_hidden.reshape(row_count, width_local)
    hidden_full = lax.all_gather(hidden_local, "tp", axis=1, tiled=True)
    normed = (rms_scale(hidden_full.astype(jnp.float32)) * input_gain.astype(jnp.float32)).astype(
        jnp.bfloat16
    )
    query_proj = jnp.dot(normed, query_weight, preferred_element_type=jnp.float32).reshape(
        row_count, query_local, head_dim
    )
    queries = rotary(rms_scale(query_proj) * query_gain.astype(jnp.float32), query_pos).astype(
        jnp.bfloat16
    )
    key_proj = jnp.dot(normed, key_weight, preferred_element_type=jnp.float32).reshape(
        row_count, kv_local, head_dim
    )
    new_keys = rotary(rms_scale(key_proj) * key_gain.astype(jnp.float32), query_pos).astype(
        jnp.bfloat16
    )
    new_values = (
        jnp.dot(normed, value_weight, preferred_element_type=jnp.float32)
        .astype(jnp.bfloat16)
        .reshape(row_count, kv_local, head_dim)
    )
    shift_pos = jnp.broadcast_to((local_base - local_start)[:, None], (slot_local, span_len))
    shifted = rotary(
        cached_keys.reshape(slot_local, span_len, kv_local, head_dim).astype(jnp.float32), shift_pos
    ).astype(jnp.bfloat16)
    slot_rows = jnp.arange(slot_local, dtype=jnp.int32)[:, None]
    joined_keys = (
        shifted.at[slot_rows, local_index]
        .set(new_keys.reshape(slot_local, select_count, kv_local, head_dim))
        .reshape(slot_local, span_len, kv_local * head_dim)
    )
    joined_values = (
        cached_values.reshape(slot_local, span_len, kv_local, head_dim)
        .at[slot_rows, local_index]
        .set(new_values.reshape(slot_local, select_count, kv_local, head_dim))
        .reshape(slot_local, span_len, kv_local * head_dim)
    )

    def attend_block(state_in, query_set, key_block, value_block, slot_id):
        query_vecs, positions, requests = query_set
        key_request, key_base, unused_start = slot_table(
            slot_id[None], slot_spans, span_order, cache_start, span_len
        )
        key_pos = key_base[0] + jnp.arange(span_len, dtype=jnp.int32)
        visible = (requests[:, None] == key_request[0]) & (key_pos[None, :] <= positions[:, None])
        run_max, run_sum, run_acc = state_in
        grouped = query_vecs.reshape(-1, kv_local, group_size, head_dim)
        key_heads = key_block.reshape(span_len, kv_local, head_dim)
        value_heads = value_block.reshape(span_len, kv_local, head_dim)
        scores = (
            jnp.einsum("qkgd,lkd->qkgl", grouped, key_heads, preferred_element_type=jnp.float32)
            * score_scale
        )
        key_mask = visible[:, None, None, :]
        scores = jnp.where(key_mask, scores, -jnp.inf)
        new_max = jnp.maximum(run_max, jnp.max(scores, axis=-1))
        safe_max = jnp.where(new_max == -jnp.inf, 0.0, new_max)
        rescale = jnp.exp(run_max - safe_max)
        weights = jnp.where(key_mask, jnp.exp(scores - safe_max[..., None]), 0.0)
        new_sum = rescale * run_sum + jnp.sum(weights, axis=-1)
        new_acc = rescale[..., None] * run_acc + jnp.einsum(
            "qkgl,lkd->qkgd",
            weights.astype(jnp.bfloat16),
            value_heads,
            preferred_element_type=jnp.float32,
        )
        return (new_max, new_sum, new_acc)

    local_set = (queries, query_pos, query_request)
    piece_keys = lax.all_gather(joined_keys, "seq", axis=0, tiled=True)
    piece_values = lax.all_gather(joined_values, "seq", axis=0, tiled=True)

    def step_slot(running, slot_item):
        block_keys, block_values, offset = slot_item
        return (attend_block(running, local_set, block_keys, block_values, offset), None)

    state_out, unused_out = lax.scan(
        step_slot,
        (
            jnp.full((row_count, kv_local, group_size), -jnp.inf, jnp.float32),
            jnp.zeros((row_count, kv_local, group_size), jnp.float32),
            jnp.zeros((row_count, kv_local, group_size, head_dim), jnp.float32),
        ),
        (piece_keys, piece_values, jnp.arange(piece_keys.shape[0], dtype=jnp.int32)),
    )
    run_max, run_sum, run_acc = state_out
    attended = (run_acc / run_sum[..., None]).astype(jnp.bfloat16)
    out_part = jnp.dot(
        attended.reshape(row_count, query_local * head_dim),
        output_weight,
        preferred_element_type=jnp.float32,
    )
    attention_sum = lax.psum(out_part.astype(jnp.bfloat16), "tp").astype(jnp.float32)
    stream = (hidden_full.astype(jnp.float32) + attention_sum).astype(jnp.bfloat16)
    normed_post = (rms_scale(stream.astype(jnp.float32)) * post_gain.astype(jnp.float32)).astype(
        jnp.bfloat16
    )
    gate_values = jnp.dot(normed_post, gate_weight, preferred_element_type=jnp.float32)
    up_values = jnp.dot(normed_post, up_weight, preferred_element_type=jnp.float32)
    active = (jax.nn.silu(gate_values) * up_values).astype(jnp.bfloat16)
    feedforward_sum = lax.psum(
        jnp.dot(active, down_weight, preferred_element_type=jnp.float32).astype(jnp.bfloat16), "tp"
    ).astype(jnp.float32)
    result_full = (stream.astype(jnp.float32) + feedforward_sum).astype(jnp.bfloat16)
    result = lax.dynamic_slice_in_dim(
        result_full, lax.axis_index("tp") * width_local, width_local, 1
    )
    return result.reshape(slot_local, select_count, width_local)


def solution(mesh):
    in_specs = (
        P("seq", None, "tp"),
        P("seq", None, "tp"),
        P("seq", None, "tp"),
        P(),
        P(),
        P(),
        P(),
        P(),
        P(None, "tp"),
        P(None, "tp"),
        P(None, "tp"),
        P(),
        P(),
        P("tp", None),
        P(),
        P(None, "tp"),
        P(None, "tp"),
        P("tp", None),
    )
    out_specs = P("seq", None, "tp")
    return jax.shard_map(
        on_device, mesh=mesh, in_specs=in_specs, out_specs=out_specs, check_vma=False
    )
```

profile of v0, /device:TPU:0, one launch (start us, length us, event | category | flops | bytes accessed | tf_op | source)
XLA Modules:
  0.0 828.0 jit_solution(6008349107138852399)
XLA Ops:
  19.5 38.6 %all_gather.9 = bf16[208,2048]{1,0:T(8,128)(2,1)S(1)} all-gather(bf16[208,256]{1,0:T(8,128)(2,1)S(1)} %bitcast.112), channel_id=1, replica_groups=mesh['seq'=16,'tp'=8] {'tp'}, dimensions={1}, use_global_device_ids=true | all-gather | bytes 958464 | tf_op jit(solution)/shard_map/all_gather | solution.py:85
  60.4 21.8 %scatter_fusion = bf16[2,1024,128]{2,1,0:T(8,128)(2,1)} fusion(bf16[2,1024,128]{2,1,0:T(8,128)(2,1)} %copy.36, s32[208]{0:T(256)S(1)} %reshape.474, bf16[208,128]{1,0:T(8,128)(2,1)S(1)} %bitcast.111), kind=kCustom, calls=%fused_computation | custom fusion | bytes 161408 | tf_op jit(solution)/shard_map/scatter | solution.py:113
  84.0 21.9 %scatter_fusion.1 = bf16[2,1024,128]{2,1,0:T(8,128)(2,1)} fusion(bf16[2,1024,128]{2,1,0:T(8,128)(2,1)} %copy.64, s32[208]{0:T(256)S(1)} %reshape.474, bf16[208,128]{1,0:T(8,128)(2,1)S(1)} %convolution_convert_fusion.2), kind=kCustom, calls=%fused_computation.1 | custom fusion | bytes 161408 | tf_op jit(solution)/shard_map/scatter | solution.py:119
  106.0 2.6 fusion.63
  112.0 24.0 %all-gather.5.cloned.1.call-done = bf16[32,1024,128]{2,1,0:T(8,128)(2,1)} async-done(((bf16[2,1024,128]{2,1,0:T(8,128)(2,1)}), bf16[32,1024,128]{2,1,0:T(8,128)(2,1)}) %all-gather.5.cloned.1.call-update) | async-done | bytes 8388624 | tf_op jit(solution)/shard_map/all_gather | solution.py:154
  135.9 54.8 %all-gather.7.cloned.1.call-done = bf16[32,1024,128]{2,1,0:T(8,128)(2,1)} async-done(((bf16[2,1024,128]{2,1,0:T(8,128)(2,1)}), bf16[32,1024,128]{2,1,0:T(8,128)(2,1)}) %all-gather.7.cloned.1.call-update) | async-done | bytes 8388624 | tf_op jit(solution)/shard_map/all_gather | solution.py:155
  190.8 436.8 %while.18 = (s32[]{:T(128)}, f32[208,1,2]{0,2,1:T(2,128)S(1)}, f32[208,1,2]{0,2,1:T(2,128)S(1)}, f32[208,1,2,128]{3,0,2,1:T(8,128)}, s32[32]{0:T(128)S(1)}, /*in...) while((s32[]{:T(128)}, f32[208,1,2]{0,2,1:T(2,128)S(1)}, ...), condition=%wide.wide.region_13.14_spmd.clone, body=%wide.wide.region_8.13_spmd.clone.sunk | while | flops 222529680 | bytes 15580799 | solution.py:161
  197.4 2.6 fusion.101
  200.0 2.1 fusion.104
  211.0 2.6 fusion.101
  213.7 2.1 fusion.104
  224.7 2.6 fusion.101
  227.3 2.1 fusion.104
  238.3 2.6 fusion.101
  241.0 2.1 fusion.104
  252.0 2.6 fusion.101
  254.6 2.1 fusion.104
  265.6 2.6 fusion.101
  268.3 2.1 fusion.104
  279.3 2.6 fusion.101
  281.9 2.1 fusion.104
  292.9 2.6 fusion.101
  295.6 2.1 fusion.104
  306.6 2.6 fusion.101
  309.2 2.1 fusion.104
  320.2 2.6 fusion.101
  322.9 2.1 fusion.104
  333.9 2.6 fusion.101
  336.5 2.1 fusion.104
  347.5 2.6 fusion.101
  350.2 2.1 fusion.104
  361.2 2.6 fusion.101
  363.8 2.1 fusion.104
  374.8 2.6 fusion.101
  377.5 2.1 fusion.104
  388.5 2.6 fusion.101
  391.1 2.1 fusion.104
  402.1 2.6 fusion.101
  404.8 2.1 fusion.104
  415.8 2.6 fusion.101
  418.4 2.1 fusion.104
  429.4 2.6 fusion.101
  432.1 2.1 fusion.104
  443.1 2.6 fusion.101
  456.7 2.6 fusion.101
  470.4 2.6 fusion.101
  484.0 2.6 fusion.101
  497.7 2.6 fusion.101
  511.3 2.6 fusion.101
  525.0 2.6 fusion.101
  538.6 2.6 fusion.101
  552.3 2.6 fusion.101
  565.9 2.6 fusion.101
  579.6 2.6 fusion.101
  593.2 2.6 fusion.101
  595.9 2.1 fusion.104
  606.9 2.6 fusion.101
  620.5 2.6 fusion.101
  628.8 2.5 convolution_convert_fusion.1
  631.4 89.7 %all-reduce.3.cloned.1.call-done = bf16[208,2048]{1,0:T(8,128)(2,1)} async-done(((bf16[208,2048]{1,0:T(8,128)(2,1)}), bf16[208,2048]{1,0:T(8,128)(2,1)}) %all-reduce.3.cloned.1.call-update) | async-done | bytes 851984 | tf_op jit(solution)/shard_map/psum | solution.py:177
  721.1 3.0 multiply_reduce_fusion
  724.1 3.7 fusion.58
  727.8 5.3 convolution_convert_fusion
  733.1 86.7 %all-reduce.5.cloned.1.call-done = bf16[208,2048]{1,0:T(8,128)(2,1)} async-done(((bf16[208,2048]{1,0:T(8,128)(2,1)}), bf16[208,2048]{1,0:T(8,128)(2,1)}) %all-reduce.5.cloned.1.call-update) | async-done | bytes 851984 | tf_op jit(solution)/shard_map/psum | solution.py:185
  (702 shorter events, 238.5 us)
Async XLA Ops:
  6.5 721.2 %copy-start = (bf16[768,2048]{1,0:T(8,128)(2,1)S(1)}, bf16[768,2048]{1,0:T(8,128)(2,1)}, u32[]{:S(2)}) copy-start(bf16[768,2048]{1,0:T(8,128)(2,1)} %param.37) | copy-start | bytes 9437188
  6.5 129.4 %all-gather.5.cloned.1.call-start = ((), (), s32[]{:S(2)}) async-start(), calls=%async_computation.2 | async-start | bytes 8912896 | tf_op jit(solution)/shard_map/all_gather | solution.py:154
  12.6 97.5 %copy-start.11 = (s32[2,104]{1,0:T(2,128)}, s32[2,104]{1,0:T(2,128)S(1)}, u32[]{:S(2)}) copy-start(s32[2,104]{1,0:T(2,128)S(1)} %get-tuple-element.392) | copy-start | bytes 2500
  15.8 3.7 copy-start.7
  16.5 41.6 %copy-start.9 = (bf16[2048]{0:T(1024)(128)(2,1)S(1)}, bf16[2048]{0:T(1024)(128)(2,1)}, u32[]{:S(2)}) copy-start(bf16[2048]{0:T(1024)(128)(2,1)} %param.27) | copy-start | bytes 12292
  16.5 41.9 %copy-start.13 = (bf16[128]{0:T(256)(128)(2,1)S(1)}, bf16[128]{0:T(256)(128)(2,1)}, u32[]{:S(2)}) copy-start(bf16[128]{0:T(256)(128)(2,1)} %param.32) | copy-start | bytes 772
  19.5 39.5 %copy-start.12 = (bf16[2048,128]{1,0:T(8,128)(2,1)S(1)}, bf16[2048,128]{1,0:T(8,128)(2,1)}, u32[]{:S(2)}) copy-start(bf16[2048,128]{1,0:T(8,128)(2,1)} %param.29) | copy-start | bytes 1572868
  82.2 23.8 %copy-start.14 = (bf16[128]{0:T(256)(128)(2,1)S(1)}, bf16[128]{0:T(256)(128)(2,1)}, u32[]{:S(2)}) copy-start(bf16[128]{0:T(256)(128)(2,1)} %param.31) | copy-start | bytes 772
  82.2 108.6 %all-gather.7.cloned.1.call-start = ((), (), s32[]{:S(2)}) async-start(), calls=%async_computation.3 | async-start | bytes 8912896 | tf_op jit(solution)/shard_map/all_gather | solution.py:155
  105.9 615.2 %all-reduce.3.cloned.1.call-start = ((), (), s32[]{:S(2)}) async-start(), calls=%async_computation | async-start | bytes 1703936 | tf_op jit(solution)/shard_map/psum | solution.py:177
  108.6 82.1 %copy-start.8 = (s32[4,8]{1,0:T(4,128)S(1)}, s32[4,8]{1,0:T(4,128)}, u32[]{:S(2)}) copy-start(s32[4,8]{1,0:T(4,128)} %param.24) | copy-start | bytes 388
  108.6 82.1 %copy-start.15 = (s32[32]{0:T(128)S(1)}, s32[32]{0:T(128)}, u32[]{:S(2)}) copy-start(s32[32]{0:T(128)} %param.23) | copy-start | bytes 388
  200.0 2.2 copy-start.1
  200.0 2.2 copy-start.5
  213.6 2.2 copy-start.1
  213.6 2.2 copy-start.5
  227.3 2.2 copy-start.1
  227.3 2.2 copy-start.5
  240.9 2.2 copy-start.1
  240.9 2.2 copy-start.5
  254.6 2.2 copy-start.1
  254.6 2.2 copy-start.5
  268.2 2.2 copy-start.1
  268.2 2.2 copy-start.5
  281.9 2.2 copy-start.1
  281.9 2.2 copy-start.5
  295.5 2.2 copy-start.1
  295.5 2.2 copy-start.5
  309.2 2.2 copy-start.1
  309.2 2.2 copy-start.5
  322.8 2.2 copy-start.1
  322.8 2.2 copy-start.5
  336.5 2.2 copy-start.1
  336.5 2.2 copy-start.5
  350.1 2.2 copy-start.1
  350.1 2.2 copy-start.5
  363.8 2.2 copy-start.1
  363.8 2.2 copy-start.5
  377.4 2.2 copy-start.1
  377.4 2.2 copy-start.5
  391.1 2.2 copy-start.5
  404.7 2.2 copy-start.5
  418.4 2.2 copy-start.5
  432.0 2.2 copy-start.5
  445.7 2.2 copy-start.5
  459.3 2.2 copy-start.5
  473.0 2.2 copy-start.5
  486.7 2.2 copy-start.5
  500.3 2.2 copy-start.5
  513.9 2.2 copy-start.1
  514.0 2.2 copy-start.5
  527.6 2.2 copy-start.5
  541.3 2.2 copy-start.5
  554.9 2.2 copy-start.1
  554.9 2.2 copy-start.5
  568.6 2.2 copy-start.5
  582.2 2.2 copy-start.5
  595.9 2.2 copy-start.5
  609.5 2.2 copy-start.5
  623.2 2.2 copy-start.5
  627.6 3.8 copy-start.10
  631.3 188.5 %all-reduce.5.cloned.1.call-start = ((), (), s32[]{:S(2)}) async-start(), calls=%async_computation.1 | async-start | bytes 1703936 | tf_op jit(solution)/shard_map/psum | solution.py:185
  721.1 3.0 copy-start.3
  721.1 3.0 copy-start.4
  (49 other events, 57.7 us)
Sparse Core Ops, SparseCore 0:
  82.3 53.5 all-gather.4
  137.7 53.0 all-gather.6
  631.4 89.5 all-reduce.2
  733.2 86.5 all-reduce.4
where the time goes:
time: 833 us; the launch traced here: 828 us
  waiting for transfers between devices  255 us (31%)
  other arithmetic  173 us (21%)
  matrix products  149 us (18%)
  local copies, waits for them, and re-layouts  101 us (12%)
  loops' own time  96.9 us (12%)
  blocking collectives  38.6 us (5%)
  between operations  13.4 us (2%)
    another operation x1, loops' own time, on_device(): lax.scan(step_slot, (jnp.full((row_count, kv_local, group_size), -jnp.inf...  96.9 us
    psum x1, waiting for transfers between devices, on_device(): lax.psum(out_part.astype(jnp.bfloat16), 'tp').astype(jnp.float32)  89.7 us
    psum x1, waiting for transfers between devices, on_device(): lax.psum(jnp.dot(active, down_weight, preferred_element_type=jnp.float32)...  86.7 us
    dot_general x32, matrix products, attend_block(): jnp.einsum('qkgd,lkd->qkgl', grouped, key_heads, preferred_element_type=j...  84.1 us
    reduce_sum x32, other arithmetic, attend_block(): new_sum = rescale * run_sum + jnp.sum(weights, axis=-1)  68.4 us
    all_gather x1, waiting for transfers between devices, on_device(): piece_values = lax.all_gather(joined_values, 'seq', axis=0, tiled=True)  54.8 us
    dot_general x32, matrix products, attend_block(): jnp.einsum('qkgl,lkd->qkgd', weights.astype(jnp.bfloat16), value_heads, p...  48.8 us
    reduce_sum x33, other arithmetic, slot_table(): span_ids = jnp.sum(slot_match * slot_spans[None, :], axis=1)  42.8 us
  transfers between devices with their start and end apart: 4, of which 4 were waited for; matrix products, arithmetic and copies ran while one was open for 4% of the time, Pallas kernels for 0%

commit v1 on v0

--- a/solution.py
+++ b/solution.py
@@ -82,7 +82,14 @@
     query_pos = (local_base[:, None] + local_index).reshape(-1)
     query_request = jnp.broadcast_to(local_request[:, None], (slot_local, select_count)).reshape(-1)
     hidden_local = selected_hidden.reshape(row_count, width_local)
-    hidden_full = lax.all_gather(hidden_local, "tp", axis=1, tiled=True)
+
+    def assign_bars(vec, mesh_dim):
+        b_next = jax.lax.axis_size(mesh_dim)
+        local_next = jnp.stack([vec] * b_next, axis=0)
+        v1 = jax.lax.all_to_all(local_next, mesh_dim, 0, 0)
+        return jnp.concatenate(v1, axis=1)
+
+    hidden_full = assign_bars(hidden_local, "tp")
     normed = (rms_scale(hidden_full.astype(jnp.float32)) * input_gain.astype(jnp.float32)).astype(
         jnp.bfloat16
     )

time: 833 us -> 799 us (0.959)
  blocking collectives: 38.6 us -> 0 us
    all_gather x1 -> x0, blocking collectives: 38.6 us -> none  [on_device(): hidden_full = lax.all_gather(hidden_local, 'tp', axis=1, tiled=True)]
  transfers between devices with their start and end apart: 4 -> 5, of which waited for: 4 -> 5; matrix products, arithmetic and copies ran while one was open for 4% -> 6% of each run, Pallas kernels for 0% -> 0%
where the time goes in v1:
time: 799 us; the launch traced here: 794 us
  waiting for transfers between devices  251 us (31%)
  other arithmetic  172 us (22%)
  matrix products  147 us (18%)
  local copies, waits for them, and re-layouts  104 us (13%)
  loops' own time  98.2 us (12%)
  between operations  13.4 us (2%)
  starting transfers between devices  8.2 us (1%)
    another operation x1, loops' own time, on_device(): lax.scan(step_slot, (jnp.full((row_count, kv_local, group_size), -jnp.inf...  98.2 us
    psum x1, waiting for transfers between devices, on_device(): lax.psum(out_part.astype(jnp.bfloat16), 'tp').astype(jnp.float32)  89.6 us
    psum x1, waiting for transfers between devices, on_device(): lax.psum(jnp.dot(active, down_weight, preferred_element_type=jnp.float32)...  86.7 us
    dot_general x32, matrix products, attend_block(): jnp.einsum('qkgd,lkd->qkgl', grouped, key_heads, preferred_element_type=j...  83.8 us
    reduce_sum x32, other arithmetic, attend_block(): new_sum = rescale * run_sum + jnp.sum(weights, axis=-1)  68.4 us
    all_gather x1, waiting for transfers between devices, on_device(): piece_values = lax.all_gather(joined_values, 'seq', axis=0, tiled=True)  54.8 us
    dot_general x32, matrix products, attend_block(): jnp.einsum('qkgl,lkd->qkgd', weights.astype(jnp.bfloat16), value_heads, p...  48.8 us
    reduce_sum x33, other arithmetic, slot_table(): span_ids = jnp.sum(slot_match * slot_spans[None, :], axis=1)  38.7 us
  transfers between devices with their start and end apart: 5, of which 5 were waited for; matrix products, arithmetic and copies ran while one was open for 6% of the time, Pallas kernels for 0%

profile of v1, /device:TPU:0, one launch (start us, length us, event | category | flops | bytes accessed | tf_op | source)
XLA Modules:
  0.0 794.1 jit_solution(5647591279669594033)
XLA Ops:
  10.5 7.9 all-to-all-start
  20.6 2.1 bitcast_convert_fusion
  23.2 2.5 fusion.36
  30.3 3.3 all-to-all-done
  38.4 21.7 %scatter_fusion = bf16[2,1024,128]{2,1,0:T(8,128)(2,1)} fusion(bf16[2,1024,128]{2,1,0:T(8,128)(2,1)} %copy.43, s32[208]{0:T(256)S(1)} %reshape.485, bf16[208,128]{1,0:T(8,128)(2,1)S(1)} %bitcast.118), kind=kCustom, calls=%fused_computation | custom fusion | bytes 161408 | tf_op jit(solution)/shard_map/scatter | solution.py:120
  62.2 21.7 %scatter_fusion.1 = bf16[2,1024,128]{2,1,0:T(8,128)(2,1)} fusion(bf16[2,1024,128]{2,1,0:T(8,128)(2,1)} %copy.71, s32[208]{0:T(256)S(1)} %reshape.485, bf16[208,128]{1,0:T(8,128)(2,1)S(1)} %convolution_convert_fusion.2), kind=kCustom, calls=%fused_computation.1 | custom fusion | bytes 161408 | tf_op jit(solution)/shard_map/scatter | solution.py:126
  84.0 2.3 copy.47
  89.4 2.2 reshape.512
  91.7 2.2 multiply_reduce_fusion.1
  94.2 16.8 %all-gather.5.cloned.1.call-done = bf16[32,1024,128]{2,1,0:T(8,128)(2,1)} async-done(((bf16[2,1024,128]{2,1,0:T(8,128)(2,1)}), bf16[32,1024,128]{2,1,0:T(8,128)(2,1)}) %all-gather.5.cloned.1.call-update) | async-done | bytes 8388624 | tf_op jit(solution)/shard_map/all_gather | solution.py:161
  111.1 54.8 %all-gather.7.cloned.1.call-done = bf16[32,1024,128]{2,1,0:T(8,128)(2,1)} async-done(((bf16[2,1024,128]{2,1,0:T(8,128)(2,1)}), bf16[32,1024,128]{2,1,0:T(8,128)(2,1)}) %all-gather.7.cloned.1.call-update) | async-done | bytes 8388624 | tf_op jit(solution)/shard_map/all_gather | solution.py:162
  165.9 429.4 %while.18 = (s32[]{:T(128)}, f32[208,1,2]{0,2,1:T(2,128)S(1)}, f32[208,1,2]{0,2,1:T(2,128)S(1)}, f32[208,1,2,128]{3,0,2,1:T(8,128)}, s32[32]{0:T(128)S(1)}, /*in...) while((s32[]{:T(128)}, f32[208,1,2]{0,2,1:T(2,128)S(1)}, ...), condition=%wide.wide.region_13.14_spmd.clone, body=%wide.wide.region_8.13_spmd.clone.sunk | while | flops 222529680 | bytes 15580799 | solution.py:168
  172.2 2.6 fusion.94
  174.9 2.1 fusion.97
  185.6 2.6 fusion.94
  188.3 2.1 fusion.97
  199.0 2.6 fusion.94
  201.7 2.1 fusion.97
  212.5 2.6 fusion.94
  215.1 2.1 fusion.97
  225.9 2.6 fusion.94
  228.5 2.1 fusion.97
  239.3 2.6 fusion.94
  241.9 2.1 fusion.97
  252.7 2.6 fusion.94
  255.4 2.1 fusion.97
  266.1 2.6 fusion.94
  268.8 2.1 fusion.97
  279.6 2.6 fusion.94
  282.2 2.1 fusion.97
  293.0 2.6 fusion.94
  295.6 2.1 fusion.97
  306.4 2.6 fusion.94
  309.0 2.1 fusion.97
  319.8 2.6 fusion.94
  322.5 2.1 fusion.97
  333.2 2.6 fusion.94
  335.9 2.1 fusion.97
  346.7 2.6 fusion.94
  349.3 2.1 fusion.97
  360.1 2.6 fusion.94
  373.5 2.6 fusion.94
  386.9 2.6 fusion.94
  400.3 2.6 fusion.94
  403.0 2.1 fusion.97
  413.8 2.6 fusion.94
  427.2 2.6 fusion.94
  440.6 2.6 fusion.94
  454.0 2.6 fusion.94
  467.4 2.6 fusion.94
  480.8 2.6 fusion.94
  494.3 2.6 fusion.94
  507.7 2.6 fusion.94
  521.1 2.6 fusion.94
  534.5 2.6 fusion.94
  547.9 2.6 fusion.94
  561.4 2.6 fusion.94
  574.8 2.6 fusion.94
  577.4 2.1 fusion.97
  588.2 2.6 fusion.94
  596.4 2.5 convolution_convert_fusion.1
  599.2 89.6 %all-reduce.3.cloned.1.call-done = bf16[208,2048]{1,0:T(8,128)(2,1)} async-done(((bf16[208,2048]{1,0:T(8,128)(2,1)}), bf16[208,2048]{1,0:T(8,128)(2,1)}) %all-reduce.3.cloned.1.call-update) | async-done | bytes 851984 | tf_op jit(solution)/shard_map/psum | solution.py:184
  693.9 5.3 convolution_convert_fusion
  699.2 86.7 %all-reduce.5.cloned.1.call-done = bf16[208,2048]{1,0:T(8,128)(2,1)} async-done(((bf16[208,2048]{1,0:T(8,128)(2,1)}), bf16[208,2048]{1,0:T(8,128)(2,1)}) %all-reduce.5.cloned.1.call-update) | async-done | bytes 851984 | tf_op jit(solution)/shard_map/psum | solution.py:192
  (708 shorter events, 242.9 us)
Async XLA Ops:
  6.5 687.3 %copy-start = (bf16[768,2048]{1,0:T(8,128)(2,1)S(1)}, bf16[768,2048]{1,0:T(8,128)(2,1)}, u32[]{:S(2)}) copy-start(bf16[768,2048]{1,0:T(8,128)(2,1)} %param.37) | copy-start | bytes 9437188
  6.5 12.0 %copy-start.8 = (s32[4,8]{1,0:T(4,128)S(1)}, s32[4,8]{1,0:T(4,128)}, u32[]{:S(2)}) copy-start(s32[4,8]{1,0:T(4,128)} %param.24) | copy-start | bytes 388
  6.5 11.9 %copy-start.12 = (s32[4,8]{1,0:T(4,128)S(1)}, s32[4,8]{1,0:T(4,128)}, u32[]{:S(2)}) copy-start(s32[4,8]{1,0:T(4,128)} %param.25) | copy-start | bytes 388
  10.5 23.1 %all-to-all-start = ((bf16[8,208,256]{2,1,0:T(8,128)(2,1)}), bf16[8,208,256]{2,1,0:T(8,128)(2,1)}, u32[]{:S(2)}, u32[]{:S(2)}) async-start(bf16[8,208,256]{2,1,0:T(8,128)(2,1)} %stack.3), calls=%async_computation | async-start | bytes 1703936 | tf_op jit(solution)/shard_map/all_to_all | solution.py:89
  18.3 4.5 copy-start.15
  18.3 92.7 %all-gather.5.cloned.1.call-start = ((), (), s32[]{:S(2)}) async-start(), calls=%async_computation.3 | async-start | bytes 8912896 | tf_op jit(solution)/shard_map/all_gather | solution.py:161
  23.2 6.2 copy-start.9
  23.2 6.2 copy-start.13
  30.2 56.1 %copy-start.11 = (s32[2,104]{1,0:T(2,128)}, s32[2,104]{1,0:T(2,128)S(1)}, u32[]{:S(2)}) copy-start(s32[2,104]{1,0:T(2,128)S(1)} %get-tuple-element.394) | copy-start | bytes 2500
  34.9 2.3 copy-start.5
  35.1 2.7 copy-start.2
  60.1 105.7 %all-gather.7.cloned.1.call-start = ((), (), s32[]{:S(2)}) async-start(), calls=%async_computation.4 | async-start | bytes 8912896 | tf_op jit(solution)/shard_map/all_gather | solution.py:162
  62.1 24.1 %copy-start.14 = (bf16[128]{0:T(256)(128)(2,1)S(1)}, bf16[128]{0:T(256)(128)(2,1)}, u32[]{:S(2)}) copy-start(bf16[128]{0:T(256)(128)(2,1)} %param.31) | copy-start | bytes 772
  83.9 604.9 %all-reduce.3.cloned.1.call-start = ((), (), s32[]{:S(2)}) async-start(), calls=%async_computation.1 | async-start | bytes 1703936 | tf_op jit(solution)/shard_map/psum | solution.py:184
  174.8 2.2 copy-start.1
  174.8 2.2 copy-start.6
  188.2 2.2 copy-start.1
  188.2 2.2 copy-start.6
  201.7 2.2 copy-start.1
  201.7 2.2 copy-start.6
  215.1 2.2 copy-start.1
  215.1 2.2 copy-start.6
  228.5 2.2 copy-start.1
  228.5 2.2 copy-start.6
  241.9 2.2 copy-start.1
  241.9 2.2 copy-start.6
  255.3 2.2 copy-start.1
  255.3 2.2 copy-start.6
  268.8 2.2 copy-start.1
  268.8 2.2 copy-start.6
  282.2 2.2 copy-start.1
  282.2 2.2 copy-start.6
  295.6 2.2 copy-start.1
  295.6 2.2 copy-start.6
  309.0 2.2 copy-start.1
  309.0 2.2 copy-start.6
  322.4 2.2 copy-start.1
  322.4 2.2 copy-start.6
  335.9 2.2 copy-start.1
  335.9 2.2 copy-start.6
  349.3 2.2 copy-start.6
  362.7 2.2 copy-start.1
  362.7 2.2 copy-start.6
  376.1 2.2 copy-start.6
  389.5 2.2 copy-start.6
  403.0 2.2 copy-start.6
  416.4 2.2 copy-start.6
  429.8 2.2 copy-start.6
  443.2 2.2 copy-start.6
  456.6 2.2 copy-start.6
  470.0 2.2 copy-start.1
  470.1 2.2 copy-start.6
  483.5 2.2 copy-start.6
  496.9 2.2 copy-start.6
  510.3 2.2 copy-start.6
  523.7 2.2 copy-start.6
  537.1 2.2 copy-start.6
  550.6 2.2 copy-start.6
  564.0 2.2 copy-start.6
  577.4 2.2 copy-start.6
  590.8 2.2 copy-start.6
  595.3 4.0 copy-start.10
  599.0 186.9 %all-reduce.5.cloned.1.call-start = ((), (), s32[]{:S(2)}) async-start(), calls=%async_computation.2 | async-start | bytes 1703936 | tf_op jit(solution)/shard_map/psum | solution.py:192
  688.8 3.3 copy-start.4
  (50 other events, 60.8 us)
Sparse Core Ops, SparseCore 0:
  60.2 50.7 all-gather.4
  112.8 53.0 all-gather.6
  599.1 89.6 all-reduce.2
  699.3 86.5 all-reduce.4
